TPU v7x, 32 devices: a whole 2x2x4 slice. The times are simulated.
32 devices in a mesh: dp: 4 (over z), cent: 8 (over y, x, core).
Axes of the slice: x: 2, y: 2, z: 4, core: 2. Of those that a mesh axis runs over, the one named last changes fastest.
Arguments:
- vectors: bfloat16 [8192, 768], P('dp'), may hold values from -30 to 30
- centroids: bfloat16 [16384, 768], P('cent'), may hold values from -1 to 1
- assignment: int32 [8192], P(('dp', 'cent')), may hold values from 0 to 16383, as said below
Outputs:
- new_centroids: bfloat16 [16384, 768], P('cent')
- row_potential: float32 [8192], P('dp')
- column_potential: float32 [16384], P('cent')
- residuals: bfloat16 [8192, 768], P(('dp', 'cent'))
Inputs may be any that keep to these rules, and one draw needn't show every extreme that they name: `assignment`: the entry's centroid is owned by index entry // 2048 of cent. In each aligned block of 256 entries (the rows of one device), at most 64 entries name centroids of one owning index; one owning index, drawn from the seed, receives exactly 64 entries from every block.
All inputs are finite; a program needn't handle non-finite values.
Results may differ from a plain program's by a relative error of at most 0.00705.
Values may be sent and summed in bfloat16 or wider, within the bound.
No kernel may reach another device: no remote copies, remote signals or barrier semaphores. Data moves between devices by JAX's collectives and lax.ppermute only.
A program may use at most 128 MiB of HBM per device.

v0:
```python
import math
import jax
import jax.numpy as jnp
from jax import lax
from jax.sharding import PartitionSpec as P

ITERS = 3
inv_temp = 2.0


def merged(value, axis, join):
    pieces = jax.tree.map(lambda part: lax.all_gather(part, axis), value)
    head = jax.tree.map(lambda part: part[0], pieces)
    tail = jax.tree.map(lambda part: part[1:], pieces)
    so_far, _ = lax.scan(lambda so_far, slab: (join(so_far, slab), None), head, tail)
    return so_far


def combine_pair(earlier, later):
    highest = jnp.maximum(earlier[0], later[0])
    return (
        highest,
        earlier[1] * jnp.exp(earlier[0] - highest) + later[1] * jnp.exp(later[0] - highest),
    )


def local_pair(shifted, axis):
    highest = jnp.max(shifted, axis=axis)
    summed = jnp.sum(jnp.exp(shifted - jnp.expand_dims(highest, axis)), axis=axis)
    return (highest, summed)


def on_device(vectors, centroids, assignment):
    row_count = vectors.shape[0]
    list_count = centroids.shape[0]
    width = vectors.shape[1]
    data_count = lax.axis_size("dp")
    owner_count = lax.axis_size("cent")
    logits = inv_temp * lax.dot_general(
        vectors, centroids, (((1,), (1,)), ((), ())), preferred_element_type=jnp.float32
    )
    log_mass = math.log(row_count * data_count / (list_count * owner_count))
    row_shift = jnp.zeros((row_count,), jnp.float32)
    column_shift = jnp.zeros((list_count,), jnp.float32)
    for iteration in range(ITERS):
        column_peak, column_total = local_pair(logits + row_shift[:, None], 0)
        column_peak, column_total = merged((column_peak, column_total), "dp", combine_pair)
        column_shift = log_mass - (column_peak + jnp.log(column_total))
        shifted = logits + column_shift[None, :]
        row_peak = lax.pmax(jnp.max(shifted, axis=1), "cent")
        row_total = lax.psum(jnp.sum(jnp.exp(shifted - row_peak[:, None]), axis=1), "cent")
        row_shift = -(row_peak + jnp.log(row_total))
    weights = jnp.exp(logits + row_shift[:, None] + column_shift[None, :]).astype(jnp.bfloat16)
    numerator = lax.dot_general(
        weights, vectors, (((0,), (0,)), ((), ())), preferred_element_type=jnp.float32
    )
    mass = jnp.sum(weights.astype(jnp.float32), axis=0)
    share_numer, share_mass = (
        lax.psum_scatter(numerator, "dp", scatter_dimension=0, tiled=True),
        lax.psum_scatter(mass, "dp", scatter_dimension=0, tiled=True),
    )
    share_rows = (share_numer / share_mass[:, None]).astype(jnp.bfloat16)
    updated = lax.all_gather(share_rows, "dp", axis=0, tiled=True)
    send_count = row_count // owner_count
    capacity = max(2, 2 * send_count // owner_count)
    sender_rows = lax.dynamic_slice_in_dim(
        vectors, lax.axis_index("cent") * send_count, send_count, 0
    )
    targets = assignment // list_count
    local_ids = assignment % list_count
    positions = jnp.arange(send_count, dtype=jnp.int32)
    earlier_same = (targets[:, None] == targets[None, :]) & (
        positions[None, :] < positions[:, None]
    )
    ranks = jnp.sum(earlier_same.astype(jnp.int32), axis=1)
    slots = targets * capacity + ranks
    outgoing = jnp.zeros((owner_count * capacity, width), jnp.bfloat16).at[slots].set(sender_rows)
    outgoing_ids = jnp.zeros((owner_count * capacity,), jnp.int32).at[slots].set(local_ids)
    outgoing = outgoing.reshape(owner_count, capacity, width)
    outgoing_ids = outgoing_ids.reshape(owner_count, capacity)
    arrived = lax.all_to_all(outgoing, "cent", split_axis=0, concat_axis=0, tiled=True)
    arrived_ids = lax.all_to_all(outgoing_ids, "cent", split_axis=0, concat_axis=0, tiled=True)
    residual_rows = (arrived.astype(jnp.float32) - updated[arrived_ids].astype(jnp.float32)).astype(
        jnp.bfloat16
    )
    returned = lax.all_to_all(residual_rows, "cent", split_axis=0, concat_axis=0, tiled=True)
    residuals = returned.reshape(owner_count * capacity, width)[slots]
    return (updated, row_shift, column_shift, residuals)


def solution(mesh):
    in_specs = (P("dp", None), P("cent", None), P(("dp", "cent")))
    out_specs = (P("cent", None), P("dp"), P("cent"), P(("dp", "cent"), None))
    return jax.shard_map(
        on_device, mesh=mesh, in_specs=in_specs, out_specs=out_specs, check_vma=False
    )
```

profile of v0, /device:TPU:0, one launch (start us, length us, event | category | flops | bytes accessed | tf_op | source)
XLA Modules:
  0.0 489.4 jit_solution(13320636421728077944)
XLA Ops:
  7.2 0.0 copy-start
  7.2 0.0 reduce-scatter.2.cloned.1.call-start
  7.2 1.8 copy-done
  9.1 11.5 %fusion.7 = (f32[2048]{0:T(1024)S(1)}, f32[2048,2048]{1,0:T(8,128)}) fusion(bf16[2048,768]{1,0:T(8,128)(2,1)S(1)} %copy-done, bf16[2048,768]{1,0:T(8,128)(2,1)} %param.10), kind=kOutput, calls=%fused_computation.55 | convolution fusion | flops 6450837504 | bytes 23076864 | tf_op jit(solution)/shard_map/dot_general | solution.py:39
  20.5 8.1 %exponential_reduce_fusion.5 = f32[2048]{0:T(1024)S(1)} fusion(f32[2048,2048]{1,0:T(8,128)} %get-tuple-element.141, f32[2048]{0:T(1024)S(1)} %get-tuple-element.140), kind=kLoop, calls=%fused_computation.20 | loop fusion | flops 8386560 | bytes 16793600 | tf_op jit(solution)/shard_map/reduce_sum | solution.py:29
  28.6 14.8 %all-gather.1 = f32[8192]{0:T(1024)S(1)} all-gather(f32[2048]{0:T(1024)S(1)} %exponential_reduce_fusion.5), channel_id=3, replica_groups=mesh['dp'=4,'cent'=8] {'dp'}, dimensions={0}, use_global_device_ids=true | all-gather | bytes 40960 | tf_op jit(solution)/shard_map/all_gather | solution.py:12
  43.5 13.2 %all-gather = f32[8192]{0:T(1024)S(1)} all-gather(f32[2048]{0:T(1024)S(1)} %get-tuple-element.140), channel_id=2, replica_groups=mesh['dp'=4,'cent'=8] {'dp'}, dimensions={0}, use_global_device_ids=true | all-gather | bytes 40960 | tf_op jit(solution)/shard_map/all_gather | solution.py:12
  56.6 0.2 while.36
  56.9 6.9 %add_reduce_fusion.4 = f32[2048]{0:T(1024)S(1)} fusion(f32[2048,2048]{1,0:T(8,128)} %get-tuple-element.141, f32[2048]{0:T(1024)S(1)} %add_subtract_fusion.2), kind=kLoop, calls=%fused_computation.25 | loop fusion | flops 8386560 | bytes 16793600 | tf_op jit(solution)/shard_map/reduce_max | solution.py:50
  63.8 12.1 %pmax.21 = f32[2048]{0:T(1024)S(1)} all-reduce(f32[2048]{0:T(1024)S(1)} %add_reduce_fusion.4), channel_id=1, replica_groups=mesh['dp'=4,'cent'=8] {'cent'}, use_global_device_ids=true, to_apply=%region_5.6 | all-reduce | flops 2048 | bytes 16384 | tf_op jit(solution)/shard_map/pmax | solution.py:50
  75.9 7.7 %exponential_reduce_fusion.4 = f32[2048]{0:T(1024)S(1)} fusion(f32[2048,2048]{1,0:T(8,128)} %get-tuple-element.141, f32[2048]{0:T(1024)S(1)} %pmax.21, f32[2048]{0:T(1024)S(1)} %add_subtract_fusion.2), kind=kLoop, calls=%fused_computation.19 | loop fusion | flops 12580864 | bytes 16801792 | tf_op jit(solution)/shard_map/reduce_sum | solution.py:51
  83.6 12.1 %psum.21 = f32[2048]{0:T(1024)S(1)} all-reduce(f32[2048]{0:T(1024)S(1)} %exponential_reduce_fusion.4), channel_id=1, replica_groups=mesh['dp'=4,'cent'=8] {'cent'}, use_global_device_ids=true, to_apply=%region_7.8 | all-reduce | flops 2048 | bytes 16384 | tf_op jit(solution)/shard_map/psum | solution.py:51
  95.7 6.9 %add_reduce_fusion.3 = f32[2048]{0:T(1024)S(1)} fusion(f32[2048,2048]{1,0:T(8,128)} %get-tuple-element.141, f32[2048]{0:T(1024)S(1)} %add_negate_fusion.2), kind=kLoop, calls=%fused_computation.24 | loop fusion | flops 8386560 | bytes 16793600 | tf_op jit(solution)/shard_map/reduce_max | solution.py:28
  102.6 7.6 %exponential_reduce_fusion.3 = f32[2048]{0:T(1024)S(1)} fusion(f32[2048,2048]{1,0:T(8,128)} %get-tuple-element.141, f32[2048]{0:T(1024)S(1)} %add_reduce_fusion.3, f32[2048]{0:T(1024)S(1)} %add_negate_fusion.2), kind=kLoop, calls=%fused_computation.18 | loop fusion | flops 12580864 | bytes 16801792 | tf_op jit(solution)/shard_map/reduce_sum | solution.py:29
  110.3 13.1 %all-gather.2 = f32[8192]{0:T(1024)S(1)} all-gather(f32[2048]{0:T(1024)S(1)} %add_reduce_fusion.3), channel_id=4, replica_groups=mesh['dp'=4,'cent'=8] {'dp'}, dimensions={0}, use_global_device_ids=true | all-gather | bytes 40960 | tf_op jit(solution)/shard_map/all_gather | solution.py:12
  123.4 13.2 %all-gather.3 = f32[8192]{0:T(1024)S(1)} all-gather(f32[2048]{0:T(1024)S(1)} %exponential_reduce_fusion.3), channel_id=5, replica_groups=mesh['dp'=4,'cent'=8] {'dp'}, dimensions={0}, use_global_device_ids=true | all-gather | bytes 40960 | tf_op jit(solution)/shard_map/all_gather | solution.py:12
  136.6 0.2 while.37
  136.8 6.9 %add_reduce_fusion.2 = f32[2048]{0:T(1024)S(1)} fusion(f32[2048,2048]{1,0:T(8,128)} %get-tuple-element.141, f32[2048]{0:T(1024)S(1)} %add_subtract_fusion.1), kind=kLoop, calls=%fused_computation.23 | loop fusion | flops 8386560 | bytes 16793600 | tf_op jit(solution)/shard_map/reduce_max | solution.py:50
  143.8 12.0 %pmax.22 = f32[2048]{0:T(1024)S(1)} all-reduce(f32[2048]{0:T(1024)S(1)} %add_reduce_fusion.2), channel_id=1, replica_groups=mesh['dp'=4,'cent'=8] {'cent'}, use_global_device_ids=true, to_apply=%region_13.14 | all-reduce | flops 2048 | bytes 16384 | tf_op jit(solution)/shard_map/pmax | solution.py:50
  155.8 7.7 %exponential_reduce_fusion.2 = f32[2048]{0:T(1024)S(1)} fusion(f32[2048,2048]{1,0:T(8,128)} %get-tuple-element.141, f32[2048]{0:T(1024)S(1)} %pmax.22, f32[2048]{0:T(1024)S(1)} %add_subtract_fusion.1), kind=kLoop, calls=%fused_computation.17 | loop fusion | flops 12580864 | bytes 16801792 | tf_op jit(solution)/shard_map/reduce_sum | solution.py:51
  163.5 12.2 %psum.22 = f32[2048]{0:T(1024)S(1)} all-reduce(f32[2048]{0:T(1024)S(1)} %exponential_reduce_fusion.2), channel_id=1, replica_groups=mesh['dp'=4,'cent'=8] {'cent'}, use_global_device_ids=true, to_apply=%region_15.16 | all-reduce | flops 2048 | bytes 16384 | tf_op jit(solution)/shard_map/psum | solution.py:51
  175.8 6.9 %add_reduce_fusion.1 = f32[2048]{0:T(1024)S(1)} fusion(f32[2048,2048]{1,0:T(8,128)} %get-tuple-element.141, f32[2048]{0:T(1024)S(1)} %add_negate_fusion.1), kind=kLoop, calls=%fused_computation.22 | loop fusion | flops 8386560 | bytes 16793600 | tf_op jit(solution)/shard_map/reduce_max | solution.py:28
  182.7 7.6 %exponential_reduce_fusion.1 = f32[2048]{0:T(1024)S(1)} fusion(f32[2048,2048]{1,0:T(8,128)} %get-tuple-element.141, f32[2048]{0:T(1024)S(1)} %add_reduce_fusion.1, f32[2048]{0:T(1024)S(1)} %add_negate_fusion.1), kind=kLoop, calls=%fused_computation.16 | loop fusion | flops 12580864 | bytes 16801792 | tf_op jit(solution)/shard_map/reduce_sum | solution.py:29
  190.3 13.1 %all-gather.4 = f32[8192]{0:T(1024)S(1)} all-gather(f32[2048]{0:T(1024)S(1)} %add_reduce_fusion.1), channel_id=6, replica_groups=mesh['dp'=4,'cent'=8] {'dp'}, dimensions={0}, use_global_device_ids=true | all-gather | bytes 40960 | tf_op jit(solution)/shard_map/all_gather | solution.py:12
  203.4 13.2 %all-gather.5 = f32[8192]{0:T(1024)S(1)} all-gather(f32[2048]{0:T(1024)S(1)} %exponential_reduce_fusion.1), channel_id=7, replica_groups=mesh['dp'=4,'cent'=8] {'dp'}, dimensions={0}, use_global_device_ids=true | all-gather | bytes 40960 | tf_op jit(solution)/shard_map/all_gather | solution.py:12
  216.7 0.2 while.38
  216.9 0.0 copy-start.1
  216.9 6.9 %add_reduce_fusion = f32[2048]{0:T(1024)S(1)} fusion(f32[2048,2048]{1,0:T(8,128)} %get-tuple-element.141, f32[2048]{0:T(1024)S(1)} %add_subtract_fusion), kind=kLoop, calls=%fused_computation.21 | loop fusion | flops 8386560 | bytes 16793600 | tf_op jit(solution)/shard_map/reduce_max | solution.py:50
  223.8 12.0 %pmax.23 = f32[2048]{0:T(1024)S(1)} all-reduce(f32[2048]{0:T(1024)S(1)} %add_reduce_fusion), channel_id=1, replica_groups=mesh['dp'=4,'cent'=8] {'cent'}, use_global_device_ids=true, to_apply=%region_21.22 | all-reduce | flops 2048 | bytes 16384 | tf_op jit(solution)/shard_map/pmax | solution.py:50
  235.9 7.7 %exponential_reduce_fusion = f32[2048]{0:T(1024)S(1)} fusion(f32[2048,2048]{1,0:T(8,128)} %get-tuple-element.141, f32[2048]{0:T(1024)S(1)} %pmax.23, f32[2048]{0:T(1024)S(1)} %add_subtract_fusion), kind=kLoop, calls=%fused_computation.15 | loop fusion | flops 12580864 | bytes 16801792 | tf_op jit(solution)/shard_map/reduce_sum | solution.py:51
  243.6 12.0 %psum.23 = f32[2048]{0:T(1024)S(1)} all-reduce(f32[2048]{0:T(1024)S(1)} %exponential_reduce_fusion), channel_id=1, replica_groups=mesh['dp'=4,'cent'=8] {'cent'}, use_global_device_ids=true, to_apply=%region_23.24 | all-reduce | flops 2048 | bytes 16384 | tf_op jit(solution)/shard_map/psum | solution.py:51
  255.6 0.0 copy-done.1
  255.6 0.0 copy-start.2
  255.7 8.0 %convert_reduce_fusion = (f32[2048]{0:T(1024)S(1)}, bf16[2048,2048]{1,0:T(8,128)(2,1)S(1)}) fusion(f32[2048]{0:T(1024)S(1)} %add_subtract_fusion, f32[2048,2048]{1,0:T(8,128)} %get-tuple-element.141, f32[2048]{0:T(1024)S(1)} %add_negate_fusion), kind=kLoop, calls=%fused_computation.13 | loop fusion | flops 20969472 | bytes 25190400 | tf_op jit(solution)/shard_map/reduce_sum | solution.py:57
  263.6 0.0 copy-start.4
  263.6 0.0 copy-start.3
  263.6 9.0 %fusion.8 = f32[2048,768]{1,0:T(8,128)} fusion(bf16[2048,2048]{1,0:T(8,128)(2,1)S(1)} %get-tuple-element.131, bf16[2048,768]{1,0:T(8,128)(2,1)S(1)} %copy-done), kind=kOutput, calls=%fused_computation.56 | convolution fusion | flops 6442450944 | bytes 17825792 | tf_op jit(solution)/shard_map/dot_general | solution.py:54
  272.6 0.0 copy-done.2
  272.6 0.0 reduce-scatter.2.cloned.1.call-update
  272.6 0.0 all-gather.8.cloned.1.call-start
  272.7 0.0 copy-done.4
  272.7 0.6 dynamic-slice
  273.9 12.4 %all-reduce = f32[2048]{0:T(1024)S(1)} all-reduce(f32[2048]{0:T(1024)S(1)} %get-tuple-element.130), channel_id=9, replica_groups=mesh['dp'=4,'cent'=8] {'dp'}, use_global_device_ids=true, to_apply=%region_26.27.clone | all-reduce | flops 2048 | bytes 16384
  286.4 0.1 dynamic-slice.1
  286.5 97.8 %reduce-scatter.2.cloned.1.call-done = f32[512,768]{1,0:T(8,128)} async-done(((f32[2048,768]{1,0:T(8,128)}), f32[512,768]{1,0:T(8,128)}) %reduce-scatter.2.cloned.1.call-update) | async-done | bytes 1572880 | tf_op jit(solution)/shard_map/reduce_scatter | solution.py:59
  384.3 2.5 divide_convert_fusion
  386.7 0.0 all-gather.8.cloned.1.call-update
  386.7 0.0 copy-done.3
  386.8 0.2 convert_reduce_fusion.1
  387.0 1.4 scatter_custom_fusion.1
  388.4 0.7 all_to_all.15
  389.0 3.7 all-to-all-start.1
  392.7 2.6 scatter_custom_fusion
  395.3 2.0 all-to-all-done.1
  397.3 4.2 all-to-all-start
  401.6 0.1 reshape.65
  401.6 49.1 %all-gather.8.cloned.1.call-done = bf16[2048,768]{1,0:T(8,128)(2,1)} async-done(((bf16[512,768]{1,0:T(8,128)(2,1)}), bf16[2048,768]{1,0:T(8,128)(2,1)}) %all-gather.8.cloned.1.call-update) | async-done | bytes 3145744 | tf_op jit(solution)/shard_map/all_gather | solution.py:63
  450.8 5.4 %gather_fusion = bf16[512,768]{1,0:T(8,128)(2,1)} fusion(bf16[2048,768]{1,0:T(8,128)(2,1)} %all-gather.8.cloned.1.call-done, s32[1024]{0:T(1024)S(1)} %pad_clamp_fusion.1), kind=kCustom, calls=%fused_computation | custom fusion | bytes 1574912 | tf_op jit(solution)/shard_map/gather | solution.py:83
  456.2 0.0 all-to-all-done
  456.2 2.4 fusion
  458.6 4.2 all-to-all-start.2
  462.8 12.6 %all-to-all-done.2 = bf16[8,64,768]{2,1,0:T(8,128)(2,1)} async-done(((bf16[8,64,768]{2,1,0:T(8,128)(2,1)}), bf16[8,64,768]{2,1,0:T(8,128)(2,1)}, u32[]{:S(2)}, u32[]{:S(2)}) %all-to-all-start.2) | async-done | bytes 786464 | tf_op jit(solution)/shard_map/all_to_all | solution.py:86
  475.4 3.4 gather_fusion.1
  478.8 3.8 copy.35
  (47 shorter events, 0.5 us)
Async XLA Ops:
  7.2 1.9 copy-start
  7.2 377.1 %reduce-scatter.2.cloned.1.call-start = ((), (), s32[]{:S(2)}) async-start(), calls=%async_computation.4 | async-start | bytes 7864320 | tf_op jit(solution)/shard_map/reduce_scatter | solution.py:59
  216.9 38.8 %copy-start.1 = (f32[2048]{0:T(1024)}, f32[2048]{0:T(1024)S(1)}, u32[]{:S(2)}) copy-start(f32[2048]{0:T(1024)S(1)} %add_subtract_fusion) | copy-start | bytes 24580
  255.6 17.0 %copy-start.2 = (f32[2048]{0:T(1024)}, f32[2048]{0:T(1024)S(1)}, u32[]{:S(2)}) copy-start(f32[2048]{0:T(1024)S(1)} %add_negate_fusion) | copy-start | bytes 24580
  263.6 9.1 %copy-start.4 = (u32[32]{0:T(128)S(1)}, u32[32]{0:T(128)}, u32[]{:S(2)}) copy-start(u32[32]{0:T(128)} %constant.77) | copy-start | bytes 388
  263.6 123.1 %copy-start.3 = (s32[256]{0:T(256)S(1)}, s32[256]{0:T(256)}, u32[]{:S(2)}) copy-start(s32[256]{0:T(256)} %param.11) | copy-start | bytes 3076
  272.6 178.1 %all-gather.8.cloned.1.call-start = ((), (), s32[]{:S(2)}) async-start(), calls=%async_computation.5 | async-start | bytes 3932160 | tf_op jit(solution)/shard_map/all_gather | solution.py:63
  389.0 8.3 %all-to-all-start.1 = ((s32[8,1,64]{2,1,0:T(1,128)}), s32[8,1,64]{2,1,0:T(1,128)S(1)}, u32[]{:S(2)}, u32[]{:S(2)}) async-start(s32[8,1,64]{2,1,0:T(1,128)} %all_to_all.15), calls=%async_computation.2 | async-start | bytes 8192 | tf_op jit(solution)/shard_map/all_to_all | solution.py:82
  397.3 58.8 %all-to-all-start = ((bf16[8,64,768]{2,1,0:T(8,128)(2,1)}), bf16[8,64,768]{2,1,0:T(8,128)(2,1)}, u32[]{:S(2)}, u32[]{:S(2)}) async-start(bf16[8,64,768]{2,1,0:T(8,128)(2,1)} %bitcast.30), calls=%async_computation.1 | async-start | bytes 1572864 | tf_op jit(solution)/shard_map/all_to_all | solution.py:81
  458.6 16.8 %all-to-all-start.2 = ((bf16[8,64,768]{2,1,0:T(8,128)(2,1)}), bf16[8,64,768]{2,1,0:T(8,128)(2,1)}, u32[]{:S(2)}, u32[]{:S(2)}) async-start(bf16[8,64,768]{2,1,0:T(8,128)(2,1)} %fusion), calls=%async_computation.3 | async-start | bytes 1572864 | tf_op jit(solution)/shard_map/all_to_all | solution.py:86
Sparse Core Ops, SparseCore 0:
  272.8 111.4 reduce-scatter.1
  386.9 63.8 all-gather.7
where the time goes:
time: 491 us; the launch traced here: 489 us
  blocking collectives  166 us (34%)
  waiting for transfers between devices  162 us (33%)
  other arithmetic  94.2 us (19%)
  matrix products  20.4 us (4%)
  local copies, waits for them, and re-layouts  20 us (4%)
  between operations  15 us (3%)
  starting transfers between devices  12.2 us (2%)
    reduce_scatter x1, waiting for transfers between devices, on_device(): lax.psum_scatter(numerator, 'dp', scatter_dimension=0, tiled=True)  97.8 us
    all_gather x6, blocking collectives, merged(): pieces = jax.tree.map(lambda part: lax.all_gather(part, axis), value)  80.6 us
    all_gather x1, waiting for transfers between devices, on_device(): updated = lax.all_gather(share_rows, 'dp', axis=0, tiled=True)  49.1 us
    psum x3, blocking collectives, on_device(): lax.psum(jnp.sum(jnp.exp(shifted - row_peak[:, None]), axis=1), 'cent')  36.3 us
    pmax x3, blocking collectives, on_device(): row_peak = lax.pmax(jnp.max(shifted, axis=1), 'cent')  36.2 us
    reduce_sum x3, other arithmetic, local_pair(): jnp.sum(jnp.exp(shifted - jnp.expand_dims(highest, axis)), axis=axis)  23.3 us
    reduce_sum x3, other arithmetic, on_device(): jnp.sum(jnp.exp(shifted - row_peak[:, None]), axis=1)  23.1 us
    reduce_max x3, other arithmetic, on_device(): row_peak = lax.pmax(jnp.max(shifted, axis=1), 'cent')  20.8 us
  transfers between devices with their start and end apart: 5, of which 4 were waited for; matrix products, arithmetic and copies ran while one was open for 2% of the time, Pallas kernels for 0%

commit v1 on v0

--- a/solution.py
+++ b/solution.py
@@ -60,7 +60,9 @@
         lax.psum_scatter(mass, "dp", scatter_dimension=0, tiled=True),
     )
     share_rows = (share_numer / share_mass[:, None]).astype(jnp.bfloat16)
-    updated = lax.all_gather(share_rows, "dp", axis=0, tiled=True)
+    updated = jnp.concatenate(
+        lax.all_to_all(jnp.stack([share_rows] * lax.axis_size("dp")), "dp", 0, 0), axis=0
+    )
     send_count = row_count // owner_count
     capacity = max(2, 2 * send_count // owner_count)
     sender_rows = lax.dynamic_slice_in_dim(

time: 491 us -> 518 us (1.055)
  waiting for transfers between devices: 162 us -> 178 us
    all_to_all x0 -> x1, waiting for transfers between devices: none -> 68.7 us  [on_device(): lax.all_to_all(jnp.stack([share_rows] * lax.axis_size('dp')), 'dp', 0, 0)]
    all_gather x1 -> x0, waiting for transfers between devices: 49.1 us -> none  [on_device(): updated = lax.all_gather(share_rows, 'dp', axis=0, tiled=True)]
    reduce_scatter x1, waiting for transfers between devices: 97.8 us -> 90.1 us  [on_device(): lax.psum_scatter(numerator, 'dp', scatter_dimension=0, tiled=True)]
    all_to_all x1, waiting for transfers between devices: 0.01 us -> 7.12 us  [on_device(): lax.all_to_all(outgoing, 'cent', split_axis=0, concat_axis=0, tiled=True)]
where the time goes in v1:
time: 518 us; the launch traced here: 516 us
  waiting for transfers between devices  178 us (34%)
  blocking collectives  168 us (32%)
  other arithmetic  94.2 us (18%)
  local copies, waits for them, and re-layouts  23.1 us (4%)
  matrix products  20.4 us (4%)
  starting transfers between devices  16.6 us (3%)
  between operations  15.1 us (3%)
    reduce_scatter x1, waiting for transfers between devices, on_device(): lax.psum_scatter(numerator, 'dp', scatter_dimension=0, tiled=True)  90.1 us
    all_gather x6, blocking collectives, merged(): pieces = jax.tree.map(lambda part: lax.all_gather(part, axis), value)  80.6 us
    all_to_all x1, waiting for transfers between devices, on_device(): lax.all_to_all(jnp.stack([share_rows] * lax.axis_size('dp')), 'dp', 0, 0)  68.7 us
    psum x3, blocking collectives, on_device(): lax.psum(jnp.sum(jnp.exp(shifted - row_peak[:, None]), axis=1), 'cent')  36.3 us
    pmax x3, blocking collectives, on_device(): row_peak = lax.pmax(jnp.max(shifted, axis=1), 'cent')  36.2 us
    reduce_sum x3, other arithmetic, local_pair(): jnp.sum(jnp.exp(shifted - jnp.expand_dims(highest, axis)), axis=axis)  23.3 us
    reduce_sum x3, other arithmetic, on_device(): jnp.sum(jnp.exp(shifted - row_peak[:, None]), axis=1)  23.1 us
    reduce_max x3, other arithmetic, on_device(): row_peak = lax.pmax(jnp.max(shifted, axis=1), 'cent')  20.8 us
  transfers between devices with their start and end apart: 5, of which 4 were waited for; matrix products, arithmetic and copies ran while one was open for 2% of the time, Pallas kernels for 0%

profile of v1, /device:TPU:0, one launch (start us, length us, event | category | flops | bytes accessed | tf_op | source)
XLA Modules:
  0.0 516.2 jit_solution(14550638761694796270)
XLA Ops:
  7.2 0.0 copy-start
  7.2 0.0 reduce-scatter.2.cloned.1.call-start
  7.2 1.8 copy-done
  9.1 11.5 %fusion.7 = (f32[2048]{0:T(1024)S(1)}, f32[2048,2048]{1,0:T(8,128)}) fusion(bf16[2048,768]{1,0:T(8,128)(2,1)S(1)} %copy-done, bf16[2048,768]{1,0:T(8,128)(2,1)} %param.10), kind=kOutput, calls=%fused_computation.55 | convolution fusion | flops 6450837504 | bytes 23076864 | tf_op jit(solution)/shard_map/dot_general | solution.py:39
  20.5 8.1 %exponential_reduce_fusion.5 = f32[2048]{0:T(1024)S(1)} fusion(f32[2048,2048]{1,0:T(8,128)} %get-tuple-element.141, f32[2048]{0:T(1024)S(1)} %get-tuple-element.140), kind=kLoop, calls=%fused_computation.20 | loop fusion | flops 8386560 | bytes 16793600 | tf_op jit(solution)/shard_map/reduce_sum | solution.py:29
  28.6 14.8 %all-gather.1 = f32[8192]{0:T(1024)S(1)} all-gather(f32[2048]{0:T(1024)S(1)} %exponential_reduce_fusion.5), channel_id=3, replica_groups=mesh['dp'=4,'cent'=8] {'dp'}, dimensions={0}, use_global_device_ids=true | all-gather | bytes 40960 | tf_op jit(solution)/shard_map/all_gather | solution.py:12
  43.5 13.2 %all-gather = f32[8192]{0:T(1024)S(1)} all-gather(f32[2048]{0:T(1024)S(1)} %get-tuple-element.140), channel_id=2, replica_groups=mesh['dp'=4,'cent'=8] {'dp'}, dimensions={0}, use_global_device_ids=true | all-gather | bytes 40960 | tf_op jit(solution)/shard_map/all_gather | solution.py:12
  56.6 0.2 while.36
  56.9 6.9 %add_reduce_fusion.4 = f32[2048]{0:T(1024)S(1)} fusion(f32[2048,2048]{1,0:T(8,128)} %get-tuple-element.141, f32[2048]{0:T(1024)S(1)} %add_subtract_fusion.2), kind=kLoop, calls=%fused_computation.25 | loop fusion | flops 8386560 | bytes 16793600 | tf_op jit(solution)/shard_map/reduce_max | solution.py:50
  63.8 12.1 %pmax.21 = f32[2048]{0:T(1024)S(1)} all-reduce(f32[2048]{0:T(1024)S(1)} %add_reduce_fusion.4), channel_id=1, replica_groups=mesh['dp'=4,'cent'=8] {'cent'}, use_global_device_ids=true, to_apply=%region_5.6 | all-reduce | flops 2048 | bytes 16384 | tf_op jit(solution)/shard_map/pmax | solution.py:50
  75.9 7.7 %exponential_reduce_fusion.4 = f32[2048]{0:T(1024)S(1)} fusion(f32[2048,2048]{1,0:T(8,128)} %get-tuple-element.141, f32[2048]{0:T(1024)S(1)} %pmax.21, f32[2048]{0:T(1024)S(1)} %add_subtract_fusion.2), kind=kLoop, calls=%fused_computation.19 | loop fusion | flops 12580864 | bytes 16801792 | tf_op jit(solution)/shard_map/reduce_sum | solution.py:51
  83.6 12.1 %psum.21 = f32[2048]{0:T(1024)S(1)} all-reduce(f32[2048]{0:T(1024)S(1)} %exponential_reduce_fusion.4), channel_id=1, replica_groups=mesh['dp'=4,'cent'=8] {'cent'}, use_global_device_ids=true, to_apply=%region_7.8 | all-reduce | flops 2048 | bytes 16384 | tf_op jit(solution)/shard_map/psum | solution.py:51
  95.7 6.9 %add_reduce_fusion.3 = f32[2048]{0:T(1024)S(1)} fusion(f32[2048,2048]{1,0:T(8,128)} %get-tuple-element.141, f32[2048]{0:T(1024)S(1)} %add_negate_fusion.2), kind=kLoop, calls=%fused_computation.24 | loop fusion | flops 8386560 | bytes 16793600 | tf_op jit(solution)/shard_map/reduce_max | solution.py:28
  102.6 7.6 %exponential_reduce_fusion.3 = f32[2048]{0:T(1024)S(1)} fusion(f32[2048,2048]{1,0:T(8,128)} %get-tuple-element.141, f32[2048]{0:T(1024)S(1)} %add_reduce_fusion.3, f32[2048]{0:T(1024)S(1)} %add_negate_fusion.2), kind=kLoop, calls=%fused_computation.18 | loop fusion | flops 12580864 | bytes 16801792 | tf_op jit(solution)/shard_map/reduce_sum | solution.py:29
  110.3 13.1 %all-gather.2 = f32[8192]{0:T(1024)S(1)} all-gather(f32[2048]{0:T(1024)S(1)} %add_reduce_fusion.3), channel_id=4, replica_groups=mesh['dp'=4,'cent'=8] {'dp'}, dimensions={0}, use_global_device_ids=true | all-gather | bytes 40960 | tf_op jit(solution)/shard_map/all_gather | solution.py:12
  123.4 13.2 %all-gather.3 = f32[8192]{0:T(1024)S(1)} all-gather(f32[2048]{0:T(1024)S(1)} %exponential_reduce_fusion.3), channel_id=5, replica_groups=mesh['dp'=4,'cent'=8] {'dp'}, dimensions={0}, use_global_device_ids=true | all-gather | bytes 40960 | tf_op jit(solution)/shard_map/all_gather | solution.py:12
  136.6 0.2 while.37
  136.8 6.9 %add_reduce_fusion.2 = f32[2048]{0:T(1024)S(1)} fusion(f32[2048,2048]{1,0:T(8,128)} %get-tuple-element.141, f32[2048]{0:T(1024)S(1)} %add_subtract_fusion.1), kind=kLoop, calls=%fused_computation.23 | loop fusion | flops 8386560 | bytes 16793600 | tf_op jit(solution)/shard_map/reduce_max | solution.py:50
  143.8 12.0 %pmax.22 = f32[2048]{0:T(1024)S(1)} all-reduce(f32[2048]{0:T(1024)S(1)} %add_reduce_fusion.2), channel_id=1, replica_groups=mesh['dp'=4,'cent'=8] {'cent'}, use_global_device_ids=true, to_apply=%region_13.14 | all-reduce | flops 2048 | bytes 16384 | tf_op jit(solution)/shard_map/pmax | solution.py:50
  155.8 7.7 %exponential_reduce_fusion.2 = f32[2048]{0:T(1024)S(1)} fusion(f32[2048,2048]{1,0:T(8,128)} %get-tuple-element.141, f32[2048]{0:T(1024)S(1)} %pmax.22, f32[2048]{0:T(1024)S(1)} %add_subtract_fusion.1), kind=kLoop, calls=%fused_computation.17 | loop fusion | flops 12580864 | bytes 16801792 | tf_op jit(solution)/shard_map/reduce_sum | solution.py:51
  163.5 12.2 %psum.22 = f32[2048]{0:T(1024)S(1)} all-reduce(f32[2048]{0:T(1024)S(1)} %exponential_reduce_fusion.2), channel_id=1, replica_groups=mesh['dp'=4,'cent'=8] {'cent'}, use_global_device_ids=true, to_apply=%region_15.16 | all-reduce | flops 2048 | bytes 16384 | tf_op jit(solution)/shard_map/psum | solution.py:51
  175.8 6.9 %add_reduce_fusion.1 = f32[2048]{0:T(1024)S(1)} fusion(f32[2048,2048]{1,0:T(8,128)} %get-tuple-element.141, f32[2048]{0:T(1024)S(1)} %add_negate_fusion.1), kind=kLoop, calls=%fused_computation.22 | loop fusion | flops 8386560 | bytes 16793600 | tf_op jit(solution)/shard_map/reduce_max | solution.py:28
  182.7 7.6 %exponential_reduce_fusion.1 = f32[2048]{0:T(1024)S(1)} fusion(f32[2048,2048]{1,0:T(8,128)} %get-tuple-element.141, f32[2048]{0:T(1024)S(1)} %add_reduce_fusion.1, f32[2048]{0:T(1024)S(1)} %add_negate_fusion.1), kind=kLoop, calls=%fused_computation.16 | loop fusion | flops 12580864 | bytes 16801792 | tf_op jit(solution)/shard_map/reduce_sum | solution.py:29
  190.3 13.1 %all-gather.4 = f32[8192]{0:T(1024)S(1)} all-gather(f32[2048]{0:T(1024)S(1)} %add_reduce_fusion.1), channel_id=6, replica_groups=mesh['dp'=4,'cent'=8] {'dp'}, dimensions={0}, use_global_device_ids=true | all-gather | bytes 40960 | tf_op jit(solution)/shard_map/all_gather | solution.py:12
  203.4 13.2 %all-gather.5 = f32[8192]{0:T(1024)S(1)} all-gather(f32[2048]{0:T(1024)S(1)} %exponential_reduce_fusion.1), channel_id=7, replica_groups=mesh['dp'=4,'cent'=8] {'dp'}, dimensions={0}, use_global_device_ids=true | all-gather | bytes 40960 | tf_op jit(solution)/shard_map/all_gather | solution.py:12
  216.7 0.2 while.38
  216.9 0.0 copy-start.1
  216.9 6.9 %add_reduce_fusion = f32[2048]{0:T(1024)S(1)} fusion(f32[2048,2048]{1,0:T(8,128)} %get-tuple-element.141, f32[2048]{0:T(1024)S(1)} %add_subtract_fusion), kind=kLoop, calls=%fused_computation.21 | loop fusion | flops 8386560 | bytes 16793600 | tf_op jit(solution)/shard_map/reduce_max | solution.py:50
  223.8 12.0 %pmax.23 = f32[2048]{0:T(1024)S(1)} all-reduce(f32[2048]{0:T(1024)S(1)} %add_reduce_fusion), channel_id=1, replica_groups=mesh['dp'=4,'cent'=8] {'cent'}, use_global_device_ids=true, to_apply=%region_21.22 | all-reduce | flops 2048 | bytes 16384 | tf_op jit(solution)/shard_map/pmax | solution.py:50
  235.9 7.7 %exponential_reduce_fusion = f32[2048]{0:T(1024)S(1)} fusion(f32[2048,2048]{1,0:T(8,128)} %get-tuple-element.141, f32[2048]{0:T(1024)S(1)} %pmax.23, f32[2048]{0:T(1024)S(1)} %add_subtract_fusion), kind=kLoop, calls=%fused_computation.15 | loop fusion | flops 12580864 | bytes 16801792 | tf_op jit(solution)/shard_map/reduce_sum | solution.py:51
  243.6 12.0 %psum.23 = f32[2048]{0:T(1024)S(1)} all-reduce(f32[2048]{0:T(1024)S(1)} %exponential_reduce_fusion), channel_id=1, replica_groups=mesh['dp'=4,'cent'=8] {'cent'}, use_global_device_ids=true, to_apply=%region_23.24 | all-reduce | flops 2048 | bytes 16384 | tf_op jit(solution)/shard_map/psum | solution.py:51
  255.6 0.0 copy-done.1
  255.6 0.0 copy-start.2
  255.7 8.0 %convert_reduce_fusion = (f32[2048]{0:T(1024)S(1)}, bf16[2048,2048]{1,0:T(8,128)(2,1)S(1)}) fusion(f32[2048]{0:T(1024)S(1)} %add_subtract_fusion, f32[2048,2048]{1,0:T(8,128)} %get-tuple-element.141, f32[2048]{0:T(1024)S(1)} %add_negate_fusion), kind=kLoop, calls=%fused_computation.13 | loop fusion | flops 20969472 | bytes 25190400 | tf_op jit(solution)/shard_map/reduce_sum | solution.py:57
  263.6 0.0 copy-start.3
  263.6 0.0 copy-start.4
  263.6 9.0 %fusion.8 = f32[2048,768]{1,0:T(8,128)} fusion(bf16[2048,2048]{1,0:T(8,128)(2,1)S(1)} %get-tuple-element.131, bf16[2048,768]{1,0:T(8,128)(2,1)S(1)} %copy-done), kind=kOutput, calls=%fused_computation.56 | convolution fusion | flops 6442450944 | bytes 17825792 | tf_op jit(solution)/shard_map/dot_general | solution.py:54
  272.6 0.0 copy-done.2
  272.6 0.0 reduce-scatter.2.cloned.1.call-update
  272.6 0.0 copy-done.3
  272.7 0.2 convert_reduce_fusion.1
  272.9 1.4 scatter_custom_fusion.1
  274.3 0.7 all_to_all.19
  274.9 3.3 all-to-all-start.2
  278.3 0.0 copy-done.4
  278.3 0.6 dynamic-slice
  279.5 15.0 %all-reduce = f32[2048]{0:T(1024)S(1)} all-reduce(f32[2048]{0:T(1024)S(1)} %get-tuple-element.130), channel_id=9, replica_groups=mesh['dp'=4,'cent'=8] {'dp'}, use_global_device_ids=true, to_apply=%region_26.27.clone | all-reduce | flops 2048 | bytes 16384
  294.5 0.1 dynamic-slice.1
  294.6 90.1 %reduce-scatter.2.cloned.1.call-done = f32[512,768]{1,0:T(8,128)} async-done(((f32[2048,768]{1,0:T(8,128)}), f32[512,768]{1,0:T(8,128)}) %reduce-scatter.2.cloned.1.call-update) | async-done | bytes 1572880 | tf_op jit(solution)/shard_map/reduce_scatter | solution.py:59
  384.6 2.4 divide_convert_fusion
  387.1 0.0 all-to-all-done.2
  387.1 3.0 stack.2
  390.1 4.9 all-to-all-start
  395.0 2.6 scatter_custom_fusion
  397.5 68.7 %all-to-all-done = bf16[4,512,768]{2,1,0:T(8,128)(2,1)} async-done(((bf16[4,512,768]{2,1,0:T(8,128)(2,1)}), bf16[4,512,768]{2,1,0:T(8,128)(2,1)}, u32[]{:S(2)}, u32[]{:S(2)}) %all-to-all-start) | async-done | bytes 3145760 | tf_op jit(solution)/shard_map/all_to_all | solution.py:64
  466.2 4.2 all-to-all-start.1
  470.5 0.1 reshape.71
  470.5 5.4 %gather_fusion = bf16[512,768]{1,0:T(8,128)(2,1)} fusion(bf16[2048,768]{1,0:T(8,128)(2,1)} %bitcast.6, s32[1024]{0:T(1024)S(1)} %pad_clamp_fusion.1), kind=kCustom, calls=%fused_computation | custom fusion | bytes 1574912 | tf_op jit(solution)/shard_map/gather | solution.py:85
  475.9 7.1 %all-to-all-done.1 = bf16[8,64,768]{2,1,0:T(8,128)(2,1)} async-done(((bf16[8,64,768]{2,1,0:T(8,128)(2,1)}), bf16[8,64,768]{2,1,0:T(8,128)(2,1)}, u32[]{:S(2)}, u32[]{:S(2)}) %all-to-all-start.1) | async-done | bytes 786464 | tf_op jit(solution)/shard_map/all_to_all | solution.py:83
  483.0 2.4 fusion
  485.5 4.2 all-to-all-start.3
  489.7 12.6 %all-to-all-done.3 = bf16[8,64,768]{2,1,0:T(8,128)(2,1)} async-done(((bf16[8,64,768]{2,1,0:T(8,128)(2,1)}), bf16[8,64,768]{2,1,0:T(8,128)(2,1)}, u32[]{:S(2)}, u32[]{:S(2)}) %all-to-all-start.3) | async-done | bytes 786464 | tf_op jit(solution)/shard_map/all_to_all | solution.py:88
  502.3 3.4 gather_fusion.1
  505.6 3.8 copy.35
  (47 shorter events, 0.5 us)
Async XLA Ops:
  7.2 1.9 copy-start
  7.2 377.5 %reduce-scatter.2.cloned.1.call-start = ((), (), s32[]{:S(2)}) async-start(), calls=%async_computation.5 | async-start | bytes 7864320 | tf_op jit(solution)/shard_map/reduce_scatter | solution.py:59
  216.9 38.8 %copy-start.1 = (f32[2048]{0:T(1024)}, f32[2048]{0:T(1024)S(1)}, u32[]{:S(2)}) copy-start(f32[2048]{0:T(1024)S(1)} %add_subtract_fusion) | copy-start | bytes 24580
  255.6 17.0 %copy-start.2 = (f32[2048]{0:T(1024)}, f32[2048]{0:T(1024)S(1)}, u32[]{:S(2)}) copy-start(f32[2048]{0:T(1024)S(1)} %add_negate_fusion) | copy-start | bytes 24580
  263.6 9.0 %copy-start.3 = (s32[256]{0:T(256)S(1)}, s32[256]{0:T(256)}, u32[]{:S(2)}) copy-start(s32[256]{0:T(256)} %param.11) | copy-start | bytes 3076
  263.6 14.6 %copy-start.4 = (u32[32]{0:T(128)S(1)}, u32[32]{0:T(128)}, u32[]{:S(2)}) copy-start(u32[32]{0:T(128)} %constant.77) | copy-start | bytes 388
  274.9 112.1 %all-to-all-start.2 = ((s32[8,1,64]{2,1,0:T(1,128)}), s32[8,1,64]{2,1,0:T(1,128)S(1)}, u32[]{:S(2)}, u32[]{:S(2)}) async-start(s32[8,1,64]{2,1,0:T(1,128)} %all_to_all.19), calls=%async_computation.3 | async-start | bytes 8192 | tf_op jit(solution)/shard_map/all_to_all | solution.py:84
  390.1 76.1 %all-to-all-start = ((bf16[4,512,768]{2,1,0:T(8,128)(2,1)}), bf16[4,512,768]{2,1,0:T(8,128)(2,1)}, u32[]{:S(2)}, u32[]{:S(2)}) async-start(bf16[4,512,768]{2,1,0:T(8,128)(2,1)} %stack.2), calls=%async_computation.1 | async-start | bytes 6291456 | tf_op jit(solution)/shard_map/all_to_all | solution.py:64
  466.2 16.8 %all-to-all-start.1 = ((bf16[8,64,768]{2,1,0:T(8,128)(2,1)}), bf16[8,64,768]{2,1,0:T(8,128)(2,1)}, u32[]{:S(2)}, u32[]{:S(2)}) async-start(bf16[8,64,768]{2,1,0:T(8,128)(2,1)} %bitcast.31), calls=%async_computation.2 | async-start | bytes 1572864 | tf_op jit(solution)/shard_map/all_to_all | solution.py:83
  485.5 16.8 %all-to-all-start.3 = ((bf16[8,64,768]{2,1,0:T(8,128)(2,1)}), bf16[8,64,768]{2,1,0:T(8,128)(2,1)}, u32[]{:S(2)}, u32[]{:S(2)}) async-start(bf16[8,64,768]{2,1,0:T(8,128)(2,1)} %fusion), calls=%async_computation.4 | async-start | bytes 1572864 | tf_op jit(solution)/shard_map/all_to_all | solution.py:88
Sparse Core Ops, SparseCore 0:
  272.8 111.8 reduce-scatter.1
